TPU v7x, 32 devices: a whole 2x2x4 slice. The times are simulated.
32 devices in a mesh: batch: 1, seq: 32 (over z, y, x, core).
Axes of the slice: x: 2, y: 2, z: 4, core: 2. Of those that a mesh axis runs over, the one named last changes fastest.
Arguments:
- tokens: bfloat16 [304, 262144], P('batch', 'seq'), may hold values from -6 to 6
- norm_gain: float32 [2, 304], replicated, may hold values from 0.5 to 1.5
- in_weight: bfloat16 [2, 608, 304], replicated, may hold values from -0.3125 to 0.3125
- in_bias: float32 [2, 608], replicated, may hold values from -3 to 3
- out_weight: bfloat16 [2, 304, 608], replicated, may hold values from -0.25 to 0.25
- out_bias: float32 [2, 304], replicated, may hold values from -3 to 3
Outputs:
- mixed: bfloat16 [304, 262144], P('batch', 'seq')
All inputs are finite; a program needn't handle non-finite values.
Results may differ from a plain program's by a relative error of at most 0.0056.
Values may be sent and summed in bfloat16 or wider, within the bound.
A program may use at most 64 MiB of HBM per device.

v0:
```python
import jax
import jax.numpy as jnp
from jax import lax
from jax.sharding import PartitionSpec as P

TRACK_CH = 16
TRACKS = 19
BLOCKS = 2


def shifted(value, axis, steps):
    count = lax.axis_size(axis)
    pairs = [(source, (source + steps) % count) for source in range(count)]
    return lax.ppermute(value, axis, pairs)


def mix_rows(rotated, gain, in_weight, in_bias, out_weight, out_bias):
    as_float = rotated.astype(jnp.float32)
    mean_square = jnp.mean(as_float * as_float, axis=0, keepdims=True)
    normed = (as_float * gain[:, None] * lax.rsqrt(mean_square + 1e-06)).astype(jnp.bfloat16)
    pre_act = jnp.dot(in_weight, normed, preferred_element_type=jnp.float32) + in_bias[:, None]
    active = jax.nn.gelu(pre_act, approximate=True).astype(jnp.bfloat16)
    summed = (
        as_float
        + jnp.dot(out_weight, active, preferred_element_type=jnp.float32)
        + out_bias[:, None]
    )
    return summed.astype(jnp.bfloat16)


def rotate(current, local_rows):
    short_count = 0
    while short_count + 1 < TRACKS and 2**short_count < local_rows:
        short_count = short_count + 1
    short_slab = current[TRACK_CH : (1 + short_count) * TRACK_CH].reshape(
        short_count, TRACK_CH, local_rows
    )
    pieces = [current[0:TRACK_CH]]
    bundle = jnp.concatenate(
        [short_slab[slot, :, local_rows - 2**slot :] for slot in range(short_count)], 1
    )
    received = shifted(bundle, "seq", 1)
    for slot in range(short_count):
        offset = 2**slot
        begin = offset - 1
        pieces.append(
            jnp.concatenate(
                [received[:, begin : begin + offset], short_slab[slot, :, : local_rows - offset]], 1
            )
        )
    for track_no in range(1 + short_count, TRACKS):
        offset = 2 ** (track_no - 1)
        one_track = current[track_no * TRACK_CH : (track_no + 1) * TRACK_CH]
        distance = offset // local_rows
        pieces.append(shifted(one_track, "seq", distance))
    return jnp.concatenate(pieces, 0)


def shards(tokens, norm_gain, in_weight, in_bias, out_weight, out_bias):
    local_rows = tokens.shape[1]
    current = tokens
    for block_no in range(BLOCKS):
        rotated = rotate(current, local_rows)
        current = mix_rows(
            rotated,
            norm_gain[block_no],
            in_weight[block_no],
            in_bias[block_no],
            out_weight[block_no],
            out_bias[block_no],
        )
    return current


def solution(mesh):
    return jax.shard_map(
        shards,
        mesh=mesh,
        in_specs=(P("batch", "seq"), P(), P(), P(), P(), P()),
        out_specs=P("batch", "seq"),
        check_vma=False,
    )
```

profile of v0, /device:TPU:15, one launch (start us, length us, event | category | flops | bytes accessed | tf_op | source)
XLA Modules:
  0.0 154.0 jit_solution(16397662430757031375)
XLA Ops:
  0.0 2.2 %slice.307 = bf16[208,8192]{1,0:T(8,128)(2,1)S(1)} slice(bf16[304,8192]{1,0:T(8,128)(2,1)} %param.6), slice={[16:224], [0:8192]} | slice | bytes 6815744 | tf_op jit(solution)/shard_map/slice | solution.py:35
  9.9 1.9 %concatenate.90 = bf16[16,8191]{1,0:T(8,128)(2,1)} concatenate(bf16[16,1]{1,0:T(8,128)(2,1)} %slice_bitcast_fusion.51, bf16[16,2]{1,0:T(8,128)(2,1)} %slice_bitcast_fusion.50, bf16[16,4]{1,0:T(8,128)(2,1)} %slice_bitcast_fusion.49, bf16[16,8]{1,0:T(8,128)(2,1)} %slice_bitcast_fusion.48, bf16[16,16]{1,0:T(8,128)(2,1)} %slice_bitcast_fusion.47, ...), dimensions={1} | concatenate | bytes 524224 | tf_op jit(solution)/shard_map/concatenate | solution.py:39
  11.9 1.8 %collective-permute-start = (bf16[16,8191]{1,0:T(8,128)(2,1)}, bf16[16,8191]{1,0:T(8,128)(2,1)S(1)}, u32[]{:S(2)}, u32[]{:S(2)}) collective-permute-start(bf16[16,8191]{1,0:T(8,128)(2,1)} %concatenate.90), channel_id=1, source_target_pairs={{0,1},{1,2},{2,3},{3,4},{4,5},{5,6},{6,7},{7,8},{8,9},{9,10},{10,1... | collective-permute-start | bytes 786344 | tf_op jit(solution)/shard_map/ppermute | solution.py:14
  23.6 21.6 %collective-permute-done.1 = bf16[16,8192]{1,0:T(8,128)(2,1)S(1)} collective-permute-done((bf16[16,8192]{1,0:T(8,128)(2,1)S(1)}, bf16[16,8192]{1,0:T(8,128)(2,1)S(1)}, u32[]{:S(2)}, u32[]{:S(2)}) %collective-permute-start.1) | collective-permute-done | bytes 262176 | tf_op jit(solution)/shard_map/ppermute | solution.py:14
  45.3 2.9 %collective-permute-done.4 = bf16[16,8192]{1,0:T(8,128)(2,1)S(1)} collective-permute-done((bf16[16,8192]{1,0:T(8,128)(2,1)S(1)}, bf16[16,8192]{1,0:T(8,128)(2,1)S(1)}, u32[]{:S(2)}, u32[]{:S(2)}) %collective-permute-start.4) | collective-permute-done | bytes 262176 | tf_op jit(solution)/shard_map/ppermute | solution.py:14
  48.2 2.3 %copy-done = bf16[304,8192]{1,0:T(8,128)(2,1)} copy-done((bf16[304,8192]{1,0:T(8,128)(2,1)}, bf16[304,8192]{1,0:T(8,128)(2,1)S(1)}, u32[]{:S(2)}) %copy-start) | copy-done | bytes 4980760
  51.6 17.6 %fusion.19 = bf16[304,8192]{1,0:T(8,128)(2,1)} fusion(bf16[304,8192]{1,0:T(8,128)(2,1)} %copy-done, f32[608]{0:T(1024)S(1)} %get-tuple-element.6, f32[304]{0:T(512)S(1)} %get-tuple-element.10, f32[8192]{0:T(1024)S(1)} %add_rsqrt_fusion.1, f32[304]{0:T(512)S(1)} %get-tuple-element.27, bf16[2,304,608]{2,1,0:T(8,128)(2,1)S(1)} %copy-done.9, ...), kind=kOutput, calls=%fused_computation.29 | convolution fusion | flops 6126305280 | bytes 15761408 | tf_op jit(solution)/shard_map/dot_general | solution.py:25
  69.1 2.2 %slice.448 = bf16[208,8192]{1,0:T(8,128)(2,1)S(1)} slice(bf16[304,8192]{1,0:T(8,128)(2,1)} %fusion.19), slice={[16:224], [0:8192]} | slice | bytes 6815744 | tf_op jit(solution)/shard_map/slice | solution.py:35
  87.0 2.5 %fusion.58 = (bf16[16,8192]{1,0:T(8,128)(2,1)}, bf16[16,8192]{1,0:T(8,128)(2,1)}, bf16[16,8192]{1,0:T(8,128)(2,1)}, bf16[16,8192]{1,0:T(8,128)(2,1)}, bf16[16,8192]{1,0:T(8,128)(2,1)}, /*index=5*/bf16[304,8192]{1,0:T(8,128)(2,1)}) fusion(bf16[304,8192]{1,0:T(8,128)(2,1)} %fusion.19), kind=kLoop, calls=%fused_computation.154 | loop fusion | bytes 3145728 | tf_op jit(solution)/shard_map/slice | solution.py:53
  89.5 1.9 %concatenate.105 = bf16[16,8191]{1,0:T(8,128)(2,1)} concatenate(bf16[16,1]{1,0:T(8,128)(2,1)} %slice_bitcast_fusion.43, bf16[16,2]{1,0:T(8,128)(2,1)} %slice_bitcast_fusion.42, bf16[16,4]{1,0:T(8,128)(2,1)} %slice_bitcast_fusion.41, bf16[16,8]{1,0:T(8,128)(2,1)} %slice_bitcast_fusion.40, bf16[16,16]{1,0:T(8,128)(2,1)} %slice_bitcast_fusion.39, ...), dimensions={1} | concatenate | bytes 524224 | tf_op jit(solution)/shard_map/concatenate | solution.py:39
  92.9 2.1 %collective-permute-start.10 = (bf16[16,8192]{1,0:T(8,128)(2,1)}, bf16[16,8192]{1,0:T(8,128)(2,1)S(1)}, u32[]{:S(2)}, u32[]{:S(2)}) collective-permute-start(bf16[16,8192]{1,0:T(8,128)(2,1)} %get-tuple-element.12), channel_id=1, source_target_pairs={{0,8},{1,9},{2,10},{3,11},{4,12},{5,13},{6,14},{7,15},{8,16},{9,17... | collective-permute-start | bytes 786440 | tf_op jit(solution)/shard_map/ppermute | solution.py:14
  95.0 2.6 %collective-permute-start.8 = (bf16[16,8192]{1,0:T(8,128)(2,1)}, bf16[16,8192]{1,0:T(8,128)(2,1)S(1)}, u32[]{:S(2)}, u32[]{:S(2)}) collective-permute-start(bf16[16,8192]{1,0:T(8,128)(2,1)} %get-tuple-element.14), channel_id=1, source_target_pairs={{0,2},{1,3},{2,4},{3,5},{4,6},{5,7},{6,8},{7,9},{8,10},{9,11},{10,... | collective-permute-start | bytes 786440 | tf_op jit(solution)/shard_map/ppermute | solution.py:14
  97.7 7.2 %collective-permute-done.6 = bf16[16,8191]{1,0:T(8,128)(2,1)S(1)} collective-permute-done((bf16[16,8191]{1,0:T(8,128)(2,1)}, bf16[16,8191]{1,0:T(8,128)(2,1)S(1)}, u32[]{:S(2)}, u32[]{:S(2)}) %collective-permute-start.6) | collective-permute-done | bytes 262144 | tf_op jit(solution)/shard_map/ppermute | solution.py:14
  104.9 4.7 %collective-permute-start.7 = (bf16[16,8192]{1,0:T(8,128)(2,1)}, bf16[16,8192]{1,0:T(8,128)(2,1)S(1)}, u32[]{:S(2)}, u32[]{:S(2)}) collective-permute-start(bf16[16,8192]{1,0:T(8,128)(2,1)} %get-tuple-element.15), channel_id=1, source_target_pairs={{0,1},{1,2},{2,3},{3,4},{4,5},{5,6},{6,7},{7,8},{8,9},{9,10},{10,1... | collective-permute-start | bytes 786440 | tf_op jit(solution)/shard_map/ppermute | solution.py:14
  109.7 1.8 %maximum_dynamic-update-slice_fusion.25 = bf16[304,8192]{1,0:T(8,128)(2,1)} fusion(bf16[304,8192]{1,0:T(8,128)(2,1)} %get-tuple-element.16, bf16[16,8191]{1,0:T(8,128)(2,1)} %slice_bitcast_fusion.6, bf16[16,1]{1,0:T(8,128)(2,1)S(1)} %slice.462), kind=kLoop, calls=%fused_computation.88 | loop fusion | flops 524288 | bytes 524320
  111.5 1.8 %maximum_dynamic-update-slice_fusion.24 = bf16[304,8192]{1,0:T(8,128)(2,1)} fusion(bf16[304,8192]{1,0:T(8,128)(2,1)} %maximum_dynamic-update-slice_fusion.25, bf16[16,8190]{1,0:T(8,128)(2,1)} %slice_bitcast_fusion.5, bf16[16,2]{1,0:T(8,128)(2,1)S(1)} %slice.464), kind=kLoop, calls=%fused_computation.87 | loop fusion | flops 524288 | bytes 524352
  113.4 1.8 %maximum_dynamic-update-slice_fusion.23 = bf16[304,8192]{1,0:T(8,128)(2,1)} fusion(bf16[304,8192]{1,0:T(8,128)(2,1)} %maximum_dynamic-update-slice_fusion.24, bf16[16,8188]{1,0:T(8,128)(2,1)} %slice_bitcast_fusion.4, bf16[16,4]{1,0:T(8,128)(2,1)S(1)} %slice.466), kind=kLoop, calls=%fused_computation.86 | loop fusion | flops 524288 | bytes 524416
  115.2 1.8 %maximum_dynamic-update-slice_fusion.22 = bf16[304,8192]{1,0:T(8,128)(2,1)} fusion(bf16[304,8192]{1,0:T(8,128)(2,1)} %maximum_dynamic-update-slice_fusion.23, bf16[16,8184]{1,0:T(8,128)(2,1)} %slice_bitcast_fusion.3, bf16[16,8]{1,0:T(8,128)(2,1)S(1)} %slice.468), kind=kLoop, calls=%fused_computation.85 | loop fusion | flops 524288 | bytes 524544
  117.1 1.8 %maximum_dynamic-update-slice_fusion.21 = bf16[304,8192]{1,0:T(8,128)(2,1)} fusion(bf16[304,8192]{1,0:T(8,128)(2,1)} %maximum_dynamic-update-slice_fusion.22, bf16[16,8176]{1,0:T(8,128)(2,1)} %slice_bitcast_fusion.2, bf16[16,16]{1,0:T(8,128)(2,1)S(1)} %slice.470), kind=kLoop, calls=%fused_computation.84 | loop fusion | flops 524288 | bytes 524800
  119.0 1.8 %maximum_dynamic-update-slice_fusion.20 = bf16[304,8192]{1,0:T(8,128)(2,1)} fusion(bf16[304,8192]{1,0:T(8,128)(2,1)} %maximum_dynamic-update-slice_fusion.21, bf16[16,8160]{1,0:T(8,128)(2,1)} %slice_bitcast_fusion.1, bf16[16,32]{1,0:T(8,128)(2,1)S(1)} %slice.472), kind=kLoop, calls=%fused_computation.83 | loop fusion | flops 524288 | bytes 525312
  120.8 1.8 %maximum_dynamic-update-slice_fusion.19 = bf16[304,8192]{1,0:T(8,128)(2,1)} fusion(bf16[304,8192]{1,0:T(8,128)(2,1)} %maximum_dynamic-update-slice_fusion.20, bf16[16,8128]{1,0:T(8,128)(2,1)} %slice_bitcast_fusion, bf16[16,64]{1,0:T(8,128)(2,1)S(1)} %slice.474), kind=kLoop, calls=%fused_computation.82 | loop fusion | flops 524288 | bytes 526336
  122.7 1.7 %maximum_dynamic-update-slice_fusion.18 = bf16[304,8192]{1,0:T(8,128)(2,1)} fusion(bf16[304,8192]{1,0:T(8,128)(2,1)} %maximum_dynamic-update-slice_fusion.19, bf16[16,8064]{1,0:T(8,128)(2,1)} %slice_bitcast_fusion.14, bf16[16,128]{1,0:T(8,128)(2,1)S(1)} %slice.476), kind=kLoop, calls=%fused_computation.81 | loop fusion | flops 524288 | bytes 524288
  133.1 3.4 %fusion.25 = f32[8192]{0:T(1024)S(1)} fusion(bf16[304,8192]{1,0:T(8,128)(2,1)} %constant_dynamic-update-slice_fusion.5), kind=kLoop, calls=%fused_computation.35 | loop fusion | flops 7462912 | bytes 5013504 | tf_op jit(solution)/shard_map/reduce_sum | solution.py:19
  136.6 17.4 %fusion.18 = bf16[304,8192]{1,0:T(8,128)(2,1)} fusion(bf16[304,8192]{1,0:T(8,128)(2,1)} %constant_dynamic-update-slice_fusion.5, f32[608]{0:T(1024)S(1)} %copy-done.4, f32[304]{0:T(512)S(1)} %copy-done.7, f32[8192]{0:T(1024)S(1)} %add_rsqrt_fusion, f32[304]{0:T(512)S(1)} %copy-done.8, bf16[2,304,608]{2,1,0:T(8,128)(2,1)S(1)} %copy-done.10, ...), kind=kOutput, calls=%fused_computation.28 | convolution fusion | flops 6126305280 | bytes 15761408 | tf_op jit(solution)/shard_map/dot_general | solution.py:25
  (152 shorter events, 45.0 us)
Async XLA Ops:
  11.8 7.0 %copy-start.3 = (f32[2,608]{1,0:T(2,128)S(1)}, f32[2,608]{1,0:T(2,128)}, u32[]{:S(2)}) copy-start(f32[2,608]{1,0:T(2,128)} %param.9) | copy-start | bytes 14596
  11.9 7.7 %copy-start.5 = (f32[2,304]{1,0:T(2,128)S(1)}, f32[2,304]{1,0:T(2,128)}, u32[]{:S(2)}) copy-start(f32[2,304]{1,0:T(2,128)} %param.11) | copy-start | bytes 7300
  11.9 7.7 %copy-start.6 = (f32[2,304]{1,0:T(2,128)S(1)}, f32[2,304]{1,0:T(2,128)}, u32[]{:S(2)}) copy-start(f32[2,304]{1,0:T(2,128)} %param.7) | copy-start | bytes 7300
  11.9 8.3 %collective-permute-start = (bf16[16,8191]{1,0:T(8,128)(2,1)}, bf16[16,8191]{1,0:T(8,128)(2,1)S(1)}, u32[]{:S(2)}, u32[]{:S(2)}) collective-permute-start(bf16[16,8191]{1,0:T(8,128)(2,1)} %concatenate.90), channel_id=1, source_target_pairs={{0,1},{1,2},{2,3},{3,4},{4,5},{5,6},{6,7},{7,8},{8,9},{9,10},{10,1... | collective-permute-start | bytes 786344 | tf_op jit(solution)/shard_map/ppermute | solution.py:14
  15.1 33.0 %collective-permute-start.5 = (bf16[16,8192]{1,0:T(8,128)(2,1)S(1)}, bf16[16,8192]{1,0:T(8,128)(2,1)S(1)}, u32[]{:S(2)}, u32[]{:S(2)}) collective-permute-start(bf16[16,8192]{1,0:T(8,128)(2,1)S(1)} %get-tuple-element.17), channel_id=1, source_target_pairs={{0,16},{1,17},{2,18},{3,19},{4,20},{5,21},{6,22},{7,23},{8,24},{9,... | collective-permute-start | bytes 786440 | tf_op jit(solution)/shard_map/ppermute | solution.py:14
  15.8 29.5 %collective-permute-start.3 = (bf16[16,8192]{1,0:T(8,128)(2,1)S(1)}, bf16[16,8192]{1,0:T(8,128)(2,1)S(1)}, u32[]{:S(2)}, u32[]{:S(2)}) collective-permute-start(bf16[16,8192]{1,0:T(8,128)(2,1)S(1)} %get-tuple-element.18), channel_id=1, source_target_pairs={{0,4},{1,5},{2,6},{3,7},{4,8},{5,9},{6,10},{7,11},{8,12},{9,13},{1... | collective-permute-start | bytes 786440 | tf_op jit(solution)/shard_map/ppermute | solution.py:14
  16.5 28.7 %collective-permute-start.2 = (bf16[16,8192]{1,0:T(8,128)(2,1)S(1)}, bf16[16,8192]{1,0:T(8,128)(2,1)S(1)}, u32[]{:S(2)}, u32[]{:S(2)}) collective-permute-start(bf16[16,8192]{1,0:T(8,128)(2,1)S(1)} %get-tuple-element.19), channel_id=1, source_target_pairs={{0,2},{1,3},{2,4},{3,5},{4,6},{5,7},{6,8},{7,9},{8,10},{9,11},{10,... | collective-permute-start | bytes 786440 | tf_op jit(solution)/shard_map/ppermute | solution.py:14
  17.7 27.4 %collective-permute-start.1 = (bf16[16,8192]{1,0:T(8,128)(2,1)S(1)}, bf16[16,8192]{1,0:T(8,128)(2,1)S(1)}, u32[]{:S(2)}, u32[]{:S(2)}) collective-permute-start(bf16[16,8192]{1,0:T(8,128)(2,1)S(1)} %get-tuple-element.20), channel_id=1, source_target_pairs={{0,1},{1,2},{2,3},{3,4},{4,5},{5,6},{6,7},{7,8},{8,9},{9,10},{10,1... | collective-permute-start | bytes 786440 | tf_op jit(solution)/shard_map/ppermute | solution.py:14
  20.1 28.0 %collective-permute-start.4 = (bf16[16,8192]{1,0:T(8,128)(2,1)S(1)}, bf16[16,8192]{1,0:T(8,128)(2,1)S(1)}, u32[]{:S(2)}, u32[]{:S(2)}) collective-permute-start(bf16[16,8192]{1,0:T(8,128)(2,1)S(1)} %get-tuple-element.22), channel_id=1, source_target_pairs={{0,8},{1,9},{2,10},{3,11},{4,12},{5,13},{6,14},{7,15},{8,16},{9,17... | collective-permute-start | bytes 786440 | tf_op jit(solution)/shard_map/ppermute | solution.py:14
  23.2 28.4 %copy-start.9 = (bf16[2,304,608]{2,1,0:T(8,128)(2,1)S(1)}, bf16[2,304,608]{2,1,0:T(8,128)(2,1)}, u32[]{:S(2)}) copy-start(bf16[2,304,608]{2,1,0:T(8,128)(2,1)} %param.10) | copy-start | bytes 2217988
  23.2 28.4 %copy-start.11 = (bf16[2,608,304]{1,2,0:T(8,128)(2,1)S(1)}, bf16[2,608,304]{1,2,0:T(8,128)(2,1)}, u32[]{:S(2)}) copy-start(bf16[2,608,304]{1,2,0:T(8,128)(2,1)} %param.8) | copy-start | bytes 2217988
  91.4 34.8 %copy-start.1 = (bf16[16,7680]{1,0:T(8,128)(2,1)S(1)}, bf16[16,7680]{1,0:T(8,128)(2,1)}, u32[]{:S(2)}) copy-start(bf16[16,7680]{1,0:T(8,128)(2,1)} %slice_bitcast_fusion.18) | copy-start | bytes 737284
  91.4 35.6 %copy-start.2 = (bf16[16,7168]{1,0:T(8,128)(2,1)S(1)}, bf16[16,7168]{1,0:T(8,128)(2,1)}, u32[]{:S(2)}) copy-start(bf16[16,7168]{1,0:T(8,128)(2,1)} %slice_bitcast_fusion.20) | copy-start | bytes 688132
  91.4 13.5 %collective-permute-start.6 = (bf16[16,8191]{1,0:T(8,128)(2,1)}, bf16[16,8191]{1,0:T(8,128)(2,1)S(1)}, u32[]{:S(2)}, u32[]{:S(2)}) collective-permute-start(bf16[16,8191]{1,0:T(8,128)(2,1)} %concatenate.105), channel_id=1, source_target_pairs={{0,1},{1,2},{2,3},{3,4},{4,5},{5,6},{6,7},{7,8},{8,9},{9,10},{10,1... | collective-permute-start | bytes 786344 | tf_op jit(solution)/shard_map/ppermute | solution.py:14
  92.9 39.5 %collective-permute-start.11 = (bf16[16,8192]{1,0:T(8,128)(2,1)}, bf16[16,8192]{1,0:T(8,128)(2,1)S(1)}, u32[]{:S(2)}, u32[]{:S(2)}) collective-permute-start(bf16[16,8192]{1,0:T(8,128)(2,1)} %get-tuple-element.11), channel_id=1, source_target_pairs={{0,16},{1,17},{2,18},{3,19},{4,20},{5,21},{6,22},{7,23},{8,24},{9,... | collective-permute-start | bytes 786440 | tf_op jit(solution)/shard_map/ppermute | solution.py:14
  92.9 38.7 %collective-permute-start.10 = (bf16[16,8192]{1,0:T(8,128)(2,1)}, bf16[16,8192]{1,0:T(8,128)(2,1)S(1)}, u32[]{:S(2)}, u32[]{:S(2)}) collective-permute-start(bf16[16,8192]{1,0:T(8,128)(2,1)} %get-tuple-element.12), channel_id=1, source_target_pairs={{0,8},{1,9},{2,10},{3,11},{4,12},{5,13},{6,14},{7,15},{8,16},{9,17... | collective-permute-start | bytes 786440 | tf_op jit(solution)/shard_map/ppermute | solution.py:14
  95.0 35.8 %collective-permute-start.9 = (bf16[16,8192]{1,0:T(8,128)(2,1)}, bf16[16,8192]{1,0:T(8,128)(2,1)S(1)}, u32[]{:S(2)}, u32[]{:S(2)}) collective-permute-start(bf16[16,8192]{1,0:T(8,128)(2,1)} %get-tuple-element.13), channel_id=1, source_target_pairs={{0,4},{1,5},{2,6},{3,7},{4,8},{5,9},{6,10},{7,11},{8,12},{9,13},{1... | collective-permute-start | bytes 786440 | tf_op jit(solution)/shard_map/ppermute | solution.py:14
  95.0 35.1 %collective-permute-start.8 = (bf16[16,8192]{1,0:T(8,128)(2,1)}, bf16[16,8192]{1,0:T(8,128)(2,1)S(1)}, u32[]{:S(2)}, u32[]{:S(2)}) collective-permute-start(bf16[16,8192]{1,0:T(8,128)(2,1)} %get-tuple-element.14), channel_id=1, source_target_pairs={{0,2},{1,3},{2,4},{3,5},{4,6},{5,7},{6,8},{7,9},{8,10},{9,11},{10,... | collective-permute-start | bytes 786440 | tf_op jit(solution)/shard_map/ppermute | solution.py:14
  104.9 24.5 %collective-permute-start.7 = (bf16[16,8192]{1,0:T(8,128)(2,1)}, bf16[16,8192]{1,0:T(8,128)(2,1)S(1)}, u32[]{:S(2)}, u32[]{:S(2)}) collective-permute-start(bf16[16,8192]{1,0:T(8,128)(2,1)} %get-tuple-element.15), channel_id=1, source_target_pairs={{0,1},{1,2},{2,3},{3,4},{4,5},{5,6},{6,7},{7,8},{8,9},{9,10},{10,1... | collective-permute-start | bytes 786440 | tf_op jit(solution)/shard_map/ppermute | solution.py:14
  126.9 9.6 %copy-start.4 = (f32[608]{0:T(1024)S(1)}, f32[608]{0:T(1024)}, u32[]{:S(2)}) copy-start(f32[608]{0:T(1024)} %get-tuple-element.5) | copy-start | bytes 7300
  126.9 9.7 %copy-start.7 = (f32[304]{0:T(512)S(1)}, f32[304]{0:T(512)}, u32[]{:S(2)}) copy-start(f32[304]{0:T(512)} %get-tuple-element.9) | copy-start | bytes 3652
  126.9 9.7 %copy-start.8 = (f32[304]{0:T(512)S(1)}, f32[304]{0:T(512)}, u32[]{:S(2)}) copy-start(f32[304]{0:T(512)} %get-tuple-element.28) | copy-start | bytes 3652
  126.9 9.7 %copy-start.10 = (bf16[2,304,608]{2,1,0:T(8,128)(2,1)S(1)}, bf16[2,304,608]{2,1,0:T(8,128)(2,1)}, u32[]{:S(2)}) copy-start(bf16[2,304,608]{2,1,0:T(8,128)(2,1)} %param.10) | copy-start | bytes 2217988
  126.9 9.7 %copy-start.12 = (bf16[2,608,304]{1,2,0:T(8,128)(2,1)S(1)}, bf16[2,608,304]{1,2,0:T(8,128)(2,1)}, u32[]{:S(2)}) copy-start(bf16[2,608,304]{1,2,0:T(8,128)(2,1)} %param.8) | copy-start | bytes 2217988
  (1 other events, 2.3 us)
where the time goes:
time: 155 us; the launch traced here: 154 us
  local copies, waits for them, and re-layouts  44.9 us (29%)
  matrix products  35 us (23%)
  waiting for transfers between devices  31.8 us (21%)
  other arithmetic  24.3 us (16%)
  starting transfers between devices  17.5 us (11%)
    dot_general x2, matrix products, mix_rows(): jnp.dot(out_weight, active, preferred_element_type=jnp.float32)  35 us
    ppermute x12, waiting for transfers between devices, shifted(): return lax.ppermute(value, axis, pairs)  31.8 us
    unnamed x26, other arithmetic  19.8 us
    ppermute x12, starting transfers between devices, shifted(): return lax.ppermute(value, axis, pairs)  17.5 us
    squeeze x24, local copies, waits for them, and re-layouts, rotate(): short_slab[slot, :, local_rows - 2 ** slot:]  14.1 us
    squeeze x26, local copies, waits for them, and re-layouts, rotate(): short_slab[slot, :, :local_rows - offset]  9.48 us
    unnamed x34, local copies, waits for them, and re-layouts  5.3 us
    reduce_sum x2, other arithmetic, mix_rows(): mean_square = jnp.mean(as_float * as_float, axis=0, keepdims=True)  4.49 us
  transfers between devices with their start and end apart: 12, of which 3 were waited for; matrix products, arithmetic and copies ran while one was open for 18% of the time, Pallas kernels for 0%

commit v1 on v0

v1 whole, which is shorter than its diff:
```python
import functools

import jax
import jax.numpy as jnp
from jax import lax
from jax.experimental import pallas as pl
from jax.experimental.pallas import tpu as pltpu
from jax.sharding import PartitionSpec as P

TRACK_CH = 16
TRACKS = 19
BLOCKS = 2
LANES = 128
CHUNK = 1024
TILE = 512
MESH = pl.DeviceIdType.MESH


class Plan:
    def __init__(self, count, rows, chunk, tile):
        self.count, self.rows, self.chunk, self.tile = count, rows, chunk, tile
        self.chunks = rows // chunk
        self.short = 0
        while self.short + 1 < TRACKS and 2**self.short < rows:
            self.short += 1
        self.near = (1 + self.short) * TRACK_CH
        self.distances = [2 ** (t - 1) // rows for t in range(1 + self.short, TRACKS)]
        self.far = len(self.distances)
        self.halo = max(2 ** (self.short - 1), LANES)
        self.pieces = []
        small = sum(1 for t in range(1, 1 + self.short) if 2 ** (t - 1) < LANES)
        self.pieces.append((TRACK_CH, small * TRACK_CH, LANES, LANES, self.chunks - 1, 0))
        for t in range(1 + small, 1 + self.short):
            offset = 2 ** (t - 1)
            width = min(offset, chunk)
            for part in range(offset // width):
                from_end = offset - part * width
                source = (rows - from_end) // chunk
                self.pieces.append((t * TRACK_CH, TRACK_CH, from_end, width, source, part))
        peers = []
        for d in self.distances + [1]:
            for signed in (d, count - d):
                if signed % count and signed % count not in peers:
                    peers.append(signed % count)
        self.peers = peers


def rotated_tile(plan, ext, far, col):
    tile, halo = plan.tile, plan.halo
    parts = []
    for t in range(1 + plan.short):
        rows = pl.ds(t * TRACK_CH, TRACK_CH)
        offset = 0 if t == 0 else 2 ** (t - 1)
        if offset % LANES == 0:
            start = pl.multiple_of(halo - offset + col, LANES)
            parts.append(ext[rows, pl.ds(start, tile)].astype(jnp.float32))
        else:
            start = pl.multiple_of(halo - LANES + col, LANES)
            window = ext[rows, pl.ds(start, tile + LANES)].astype(jnp.float32)
            parts.append(pltpu.roll(window, offset, 1)[:, LANES:])
    parts.append(far[:, pl.ds(pl.multiple_of(col, LANES), tile)].astype(jnp.float32))
    return jnp.concatenate(parts, 0)


def mix_tile(as_float, gain, in_weight, in_bias, out_weight, out_bias):
    mean_square = jnp.mean(as_float * as_float, axis=0, keepdims=True)
    normed = (as_float * gain * lax.rsqrt(mean_square + 1e-06)).astype(jnp.bfloat16)
    pre_act = jnp.dot(in_weight, normed, preferred_element_type=jnp.float32) + in_bias
    inner = pre_act * (0.7978845608028654 + 0.035677408136300125 * (pre_act * pre_act))
    half = 0.5 * pre_act
    active = (half + half * jnp.tanh(inner)).astype(jnp.bfloat16)
    summed = as_float + jnp.dot(out_weight, active, preferred_element_type=jnp.float32) + out_bias
    return summed.astype(jnp.bfloat16)


def kernel(plan, tokens, gain, w_in, b_in, w_out, b_out, out,
           ext0, ext1, far0, far1, sent1, result,
           far_send, far_recv, halo_send, halo_recv, load_sem, store_sem):
    me = lax.axis_index("seq")
    chunk, tile, near, halo, rows = plan.chunk, plan.tile, plan.near, plan.halo, plan.rows
    exts, fars = (ext0, ext1), (far0, far1)

    load = pltpu.make_async_copy(tokens.at[pl.ds(0, near), :], ext0.at[:, pl.ds(halo, rows)], load_sem)
    load.start()

    barrier = pltpu.get_barrier_semaphore()
    for peer in plan.peers:
        pl.semaphore_signal(barrier, inc=1, device_id={"seq": lax.rem(me + peer, plan.count)}, device_id_type=MESH)
    pl.semaphore_wait(barrier, len(plan.peers))

    def far_copy(block, index, number):
        cols = pl.ds(pl.multiple_of(number * chunk, LANES), chunk)
        if block == 0:
            source = tokens.at[pl.ds(near + index * TRACK_CH, TRACK_CH), cols]
        else:
            source = sent1.at[pl.ds(index * TRACK_CH, TRACK_CH), cols]
        return pltpu.make_async_remote_copy(
            src_ref=source,
            dst_ref=fars[block].at[pl.ds(index * TRACK_CH, TRACK_CH), cols],
            send_sem=far_send.at[block, index, number],
            recv_sem=far_recv.at[block, index, number],
            device_id={"seq": lax.rem(me + plan.distances[index], plan.count)},
            device_id_type=MESH,
        )

    def halo_copy(block, number):
        first, height, from_end, width, _, _ = plan.pieces[number]
        if block == 0:
            source = tokens.at[pl.ds(first, height), pl.ds(rows - from_end, width)]
        else:
            source = ext1.at[pl.ds(first, height), pl.ds(halo + rows - from_end, width)]
        return pltpu.make_async_remote_copy(
            src_ref=source,
            dst_ref=exts[block].at[pl.ds(first, height), pl.ds(halo - from_end, width)],
            send_sem=halo_send.at[block, number],
            recv_sem=halo_recv.at[block, number],
            device_id={"seq": lax.rem(me + 1, plan.count)},
            device_id_type=MESH,
        )

    def store(number):
        cols = pl.ds(pl.multiple_of(number * chunk, LANES), chunk)
        return pltpu.make_async_copy(result.at[:, cols], out.at[:, cols], store_sem.at[number])

    @pl.loop(0, plan.chunks)
    def _(step):
        number = plan.chunks - 1 - step
        for index in range(plan.far):
            far_copy(0, index, number).start()
        for piece, (*_, reader) in enumerate(plan.pieces):
            @pl.when(number == reader)
            def _(piece=piece):
                halo_copy(0, piece).start()

    load.wait()

    for block in range(BLOCKS):
        ext, far = exts[block], fars[block]

        @pl.loop(0, plan.chunks)
        def _(step, block=block, ext=ext, far=far):
            number = plan.chunks - 1 - step
            for index in range(plan.far):
                far_copy(block, index, number).wait_recv()
            for piece, (*_, reader) in enumerate(plan.pieces):
                @pl.when(number == reader)
                def _(piece=piece):
                    halo_copy(block, piece).wait_recv()

            @pl.loop(0, chunk // tile)
            def _(part):
                col = pl.multiple_of(number * chunk + part * tile, LANES)
                value = mix_tile(
                    rotated_tile(plan, ext, far, col),
                    gain[block], w_in[block], b_in[block], w_out[block], b_out[block],
                )
                if block + 1 < BLOCKS:
                    ext1[:, pl.ds(pl.multiple_of(halo + col, LANES), tile)] = value[:near]
                    sent1[:, pl.ds(col, tile)] = value[near:]
                else:
                    result[:, pl.ds(col, tile)] = value

            if block + 1 < BLOCKS:
                for index in range(plan.far):
                    far_copy(1, index, number).start()
                for piece, (*_, source, _) in enumerate(plan.pieces):
                    @pl.when(number == source)
                    def _(piece=piece):
                        halo_copy(1, piece).start()
            else:
                store(number).start()

    @pl.loop(0, plan.chunks)
    def _(number):
        for block in range(BLOCKS):
            for index in range(plan.far):
                far_copy(block, index, number).wait_send()
        store(number).wait()

    for block in range(BLOCKS):
        for piece in range(len(plan.pieces)):
            halo_copy(block, piece).wait_send()


def solution(mesh):
    count = mesh.shape["seq"]

    def shards(tokens, norm_gain, in_weight, in_bias, out_weight, out_bias):
        channels, rows = tokens.shape
        plan = Plan(count, rows, min(CHUNK, rows // 2), min(TILE, rows // 2))
        distant = plan.far * TRACK_CH
        wide = plan.halo + rows
        vmem = pl.BlockSpec(memory_space=pltpu.VMEM)
        return pl.pallas_call(
            functools.partial(kernel, plan),
            out_shape=jax.ShapeDtypeStruct(tokens.shape, tokens.dtype),
            in_specs=[pl.BlockSpec(memory_space=pl.ANY)] + [vmem] * 5,
            out_specs=pl.BlockSpec(memory_space=pl.ANY),
            scratch_shapes=[
                pltpu.VMEM((plan.near, wide), jnp.bfloat16),
                pltpu.VMEM((plan.near, wide), jnp.bfloat16),
                pltpu.VMEM((distant, rows), jnp.bfloat16),
                pltpu.VMEM((distant, rows), jnp.bfloat16),
                pltpu.VMEM((distant, rows), jnp.bfloat16),
                pltpu.VMEM((channels, rows), jnp.bfloat16),
                pltpu.SemaphoreType.DMA((BLOCKS, plan.far, plan.chunks)),
                pltpu.SemaphoreType.DMA((BLOCKS, plan.far, plan.chunks)),
                pltpu.SemaphoreType.DMA((BLOCKS, len(plan.pieces))),
                pltpu.SemaphoreType.DMA((BLOCKS, len(plan.pieces))),
                pltpu.SemaphoreType.DMA,
                pltpu.SemaphoreType.DMA((plan.chunks,)),
            ],
            compiler_params=pltpu.CompilerParams(
                collective_id=0, has_side_effects=True, vmem_limit_bytes=56 * 2**20
            ),
        )(tokens, norm_gain[:, :, None], in_weight, in_bias[:, :, None], out_weight, out_bias[:, :, None])

    return jax.shard_map(
        shards,
        mesh=mesh,
        in_specs=(P("batch", "seq"), P(), P(), P(), P(), P()),
        out_specs=P("batch", "seq"),
        check_vma=False,
    )
```

time: 155 us -> 119 us (0.77)
  the two profiles are of different devices: /device:TPU:15 before, /device:TPU:7 now
where the time goes in v1:
time: 119 us
  Pallas kernels  107 us (90%)
  local copies, waits for them, and re-layouts  12.3 us (10%)
    pallas_call x1, Pallas kernels, shards(): pl.pallas_call(functools.partial(kernel, plan), out_shape=jax.ShapeDtypeS...  107 us
    unnamed x2, local copies, waits for them, and re-layouts  7.39 us

profile of v1, /device:TPU:7, one launch (start us, length us, event | category | flops | bytes accessed | tf_op | source)
XLA Modules:
  0.0 119.1 jit_solution(17606951520990463683)
XLA Ops:
  0.0 1.6 %copy.8.gain = f32[2,304,1]{2,1,0:T(8,128)} copy(f32[2,304,1]{1,0,2:T(2,128)} %bitcast.4) | data formatting | bytes 4864 | tf_op jit(solution)/shard_map/broadcast_in_dim | solution.py:216
  1.6 1.6 %copy.11.b_out = f32[2,304,1]{2,1,0:T(8,128)} copy(f32[2,304,1]{1,0,2:T(2,128)} %bitcast.5) | data formatting | bytes 4864 | tf_op jit(solution)/shard_map/broadcast_in_dim | solution.py:216
  3.1 1.8 %copy.10.b_in = f32[2,608,1]{2,1,0:T(8,128)} copy(f32[2,608,1]{1,0,2:T(2,128)} %bitcast.3) | data formatting | bytes 9728 | tf_op jit(solution)/shard_map/broadcast_in_dim | solution.py:216
  4.9 2.2 %copy.9.w_in = bf16[2,608,304]{2,1,0:T(8,128)(2,1)} copy(bf16[2,608,304]{1,2,0:T(8,128)(2,1)} %param.8) | data formatting | bytes 1478656 | tf_op args[2]
  7.1 106.8 %shard_map.64 = bf16[304,8192]{1,0:T(8,128)(2,1)} custom-call(bf16[304,8192]{1,0:T(8,128)(2,1)} %tokens.1, f32[2,304,1]{2,1,0:T(8,128)} %copy.8.gain, bf16[2,608,304]{2,1,0:T(8,128)(2,1)} %copy.9.w_in, f32[2,608,1]{2,1,0:T(8,128)} %copy.10.b_in, bf16[2,304,608]{2,1,0:T(8,128)(2,1)} %w_out.1, f32[2,304,1]{2,1,0:T(8,128)} %copy.11.b_out), custom_call_target="tpu_custom_call" | custom-call | tf_op jit(solution)/shard_map/pallas_call | solution.py:194
  113.9 5.2 %copy.13 = bf16[304,8192]{1,0:T(8,128)(2,1)} copy(bf16[304,8192]{1,0:T(8,128)(2,1)} %shard_map.64) | data formatting | bytes 9961472

commit v2 on v1

--- a/solution.py
+++ b/solution.py
@@ -12,12 +12,13 @@
 BLOCKS = 2
 LANES = 128
 CHUNK = 1024
-TILE = 512
+TILE = 1024
+LAG = 2
 MESH = pl.DeviceIdType.MESH
 
 
 class Plan:
-    def __init__(self, count, rows, chunk, tile):
+    def __init__(self, count, rows, chunk, tile, plane):
         self.count, self.rows, self.chunk, self.tile = count, rows, chunk, tile
         self.chunks = rows // chunk
         self.short = 0
@@ -37,8 +38,16 @@
                 from_end = offset - part * width
                 source = (rows - from_end) // chunk
                 self.pieces.append((t * TRACK_CH, TRACK_CH, from_end, width, source, part))
+        self.plane = plane
+        self.relays = []
+        if plane:
+            last = plane - 1
+            self.relays = [(0, last, 2, 0), (None, last, 3, 0), (1, last - 1, 0, 0), (1, last, 1, 1)]
         peers = []
-        for d in self.distances + [1]:
+        hops = [1] + self.distances
+        for _, sender, relay, receiver in self.relays:
+            hops += [(relay - sender) % count, (plane + receiver - relay) % count]
+        for d in hops:
             for signed in (d, count - d):
                 if signed % count and signed % count not in peers:
                     peers.append(signed % count)
@@ -62,6 +71,14 @@
     return jnp.concatenate(parts, 0)
 
 
+def columns(row):
+    return jnp.broadcast_to(row, (LANES, row.shape[1])).T
+
+
+def across(column, width):
+    return jnp.concatenate([column] * (width // LANES), 1)
+
+
 def mix_tile(as_float, gain, in_weight, in_bias, out_weight, out_bias):
     mean_square = jnp.mean(as_float * as_float, axis=0, keepdims=True)
     normed = (as_float * gain * lax.rsqrt(mean_square + 1e-06)).astype(jnp.bfloat16)
@@ -73,9 +90,10 @@
     return summed.astype(jnp.bfloat16)
 
 
-def kernel(plan, tokens, gain, w_in, b_in, w_out, b_out, out,
-           ext0, ext1, far0, far1, sent1, result,
-           far_send, far_recv, halo_send, halo_recv, load_sem, store_sem):
+def kernel(plan, tokens, gain_in, w_in_t, b_in_in, w_out, b_out_in, out,
+           gain, w_in, b_in, b_out, relay_far, relay_halo, ext0, ext1, far0, far1, sent1, result,
+           far_send, far_recv, halo_send, halo_recv,
+           pass_send, pass_recv, pass_halo_send, pass_halo_recv, load_sem, store_sem):
     me = lax.axis_index("seq")
     chunk, tile, near, halo, rows = plan.chunk, plan.tile, plan.near, plan.halo, plan.rows
     exts, fars = (ext0, ext1), (far0, far1)
@@ -88,35 +106,96 @@
         pl.semaphore_signal(barrier, inc=1, device_id={"seq": lax.rem(me + peer, plan.count)}, device_id_type=MESH)
     pl.semaphore_wait(barrier, len(plan.peers))
 
-    def far_copy(block, index, number):
+    place = lax.rem(me, plan.plane) if plan.plane else me
+
+    def along(hop):
+        return {"seq": lax.rem(me + hop + plan.count, plan.count)}
+
+    def far_copy(block, index, number, relay=None):
         cols = pl.ds(pl.multiple_of(number * chunk, LANES), chunk)
         if block == 0:
             source = tokens.at[pl.ds(near + index * TRACK_CH, TRACK_CH), cols]
         else:
             source = sent1.at[pl.ds(index * TRACK_CH, TRACK_CH), cols]
+        if relay is None:
+            target = fars[block].at[pl.ds(index * TRACK_CH, TRACK_CH), cols]
+            arrived, hop = far_recv.at[block, index, number], plan.distances[index]
+        else:
+            target, arrived, hop = relay_far.at[block, :, cols], pass_recv.at[block, number], relay[2] - relay[1]
         return pltpu.make_async_remote_copy(
-            src_ref=source,
+            src_ref=source, dst_ref=target, send_sem=far_send.at[block, index, number], recv_sem=arrived,
+            device_id=along(hop), device_id_type=MESH,
+        )
+
+    def far_pass(block, relay, number):
+        index, _, at, receiver = relay
+        cols = pl.ds(pl.multiple_of(number * chunk, LANES), chunk)
+        return pltpu.make_async_remote_copy(
+            src_ref=relay_far.at[block, :, cols],
             dst_ref=fars[block].at[pl.ds(index * TRACK_CH, TRACK_CH), cols],
-            send_sem=far_send.at[block, index, number],
+            send_sem=pass_send.at[block, number],
             recv_sem=far_recv.at[block, index, number],
-            device_id={"seq": lax.rem(me + plan.distances[index], plan.count)},
-            device_id_type=MESH,
+            device_id=along(plan.plane + receiver - at), device_id_type=MESH,
         )
 
-    def halo_copy(block, number):
+    def halo_copy(block, number, relay=None):
         first, height, from_end, width, _, _ = plan.pieces[number]
+        where = (pl.ds(first, height), pl.ds(halo - from_end, width))
         if block == 0:
             source = tokens.at[pl.ds(first, height), pl.ds(rows - from_end, width)]
         else:
             source = ext1.at[pl.ds(first, height), pl.ds(halo + rows - from_end, width)]
+        if relay is None:
+            target, arrived, hop = exts[block].at[where], halo_recv.at[block, number], 1
+        else:
+            target, arrived = relay_halo.at[(block, *where)], pass_halo_recv.at[block, number]
+            hop = relay[2] - relay[1]
         return pltpu.make_async_remote_copy(
-            src_ref=source,
-            dst_ref=exts[block].at[pl.ds(first, height), pl.ds(halo - from_end, width)],
-            send_sem=halo_send.at[block, number],
+            src_ref=source, dst_ref=target, send_sem=halo_send.at[block, number], recv_sem=arrived,
+            device_id=along(hop), device_id_type=MESH,
+        )
+
+    def halo_pass(block, relay, number):
+        first, height, from_end, width, _, _ = plan.pieces[number]
+        where = (pl.ds(first, height), pl.ds(halo - from_end, width))
+        return pltpu.make_async_remote_copy(
+            src_ref=relay_halo.at[(block, *where)],
+            dst_ref=exts[block].at[where],
+            send_sem=pass_halo_send.at[block, number],
             recv_sem=halo_recv.at[block, number],
-            device_id={"seq": lax.rem(me + 1, plan.count)},
-            device_id_type=MESH,
+            device_id=along(plan.plane + relay[3] - relay[2]), device_id_type=MESH,
         )
+
+    def start(make, key, *args):
+        relays = [relay for relay in plan.relays if relay[0] == key]
+        direct = place >= 0
+        for relay in relays:
+            direct = direct & (place != relay[1])
+
+            @pl.when(place == relay[1])
+            def _(relay=relay):
+                make(*args, relay=relay).start()
+
+        if relays:
+            @pl.when(direct)
+            def _():
+                make(*args).start()
+        else:
+            make(*args).start()
+
+    def forward(block, number, halo_of):
+        for relay in plan.relays:
+            @pl.when((place == relay[2]) & (number >= 0) & (number < plan.chunks))
+            def _(relay=relay):
+                if relay[0] is None:
+                    for piece in range(len(plan.pieces)):
+                        @pl.when(number == plan.pieces[piece][halo_of])
+                        def _(piece=piece):
+                            halo_copy(block, piece, relay).wait_recv()
+                            halo_pass(block, relay, piece).start()
+                else:
+                    far_copy(block, relay[0], number, relay).wait_recv()
+                    far_pass(block, relay, number).start()
 
     def store(number):
         cols = pl.ds(pl.multiple_of(number * chunk, LANES), chunk)
@@ -126,11 +205,19 @@
     def _(step):
         number = plan.chunks - 1 - step
         for index in range(plan.far):
-            far_copy(0, index, number).start()
+            start(far_copy, index, 0, index, number)
         for piece, (*_, reader) in enumerate(plan.pieces):
             @pl.when(number == reader)
             def _(piece=piece):
-                halo_copy(0, piece).start()
+                start(halo_copy, None, 0, piece)
+
+    forward(0, plan.chunks - 1, 5)
+
+    for block in range(BLOCKS):
+        gain[block] = columns(gain_in[block:block + 1, :])
+        b_in[block] = columns(b_in_in[block:block + 1, :])
+        b_out[block] = columns(b_out_in[block:block + 1, :])
+        w_in[block] = w_in_t[block].T
 
     load.wait()
 
@@ -140,6 +227,9 @@
         @pl.loop(0, plan.chunks)
         def _(step, block=block, ext=ext, far=far):
             number = plan.chunks - 1 - step
+            if block == 0:
+                forward(0, number - 1, 5)
+            forward(1, number + LAG - block * plan.chunks, 4)
             for index in range(plan.far):
                 far_copy(block, index, number).wait_recv()
             for piece, (*_, reader) in enumerate(plan.pieces):
@@ -152,7 +242,8 @@
                 col = pl.multiple_of(number * chunk + part * tile, LANES)
                 value = mix_tile(
                     rotated_tile(plan, ext, far, col),
-                    gain[block], w_in[block], b_in[block], w_out[block], b_out[block],
+                    across(gain[block], tile), w_in[block], across(b_in[block], tile),
+                    w_out[block], across(b_out[block], tile),
                 )
                 if block + 1 < BLOCKS:
                     ext1[:, pl.ds(pl.multiple_of(halo + col, LANES), tile)] = value[:near]
@@ -162,11 +253,11 @@
 
             if block + 1 < BLOCKS:
                 for index in range(plan.far):
-                    far_copy(1, index, number).start()
+                    start(far_copy, index, 1, index, number)
                 for piece, (*_, source, _) in enumerate(plan.pieces):
                     @pl.when(number == source)
                     def _(piece=piece):
-                        halo_copy(1, piece).start()
+                        start(halo_copy, None, 1, piece)
             else:
                 store(number).start()
 
@@ -175,19 +266,41 @@
         for block in range(BLOCKS):
             for index in range(plan.far):
                 far_copy(block, index, number).wait_send()
+            for relay in plan.relays:
+                if relay[0] is not None:
+                    @pl.when(place == relay[2])
+                    def _(relay=relay, block=block):
+                        far_pass(block, relay, number).wait_send()
         store(number).wait()
 
     for block in range(BLOCKS):
         for piece in range(len(plan.pieces)):
             halo_copy(block, piece).wait_send()
+            for relay in plan.relays:
+                if relay[0] is None:
+                    @pl.when(place == relay[2])
+                    def _(relay=relay, block=block, piece=piece):
+                        halo_pass(block, relay, piece).wait_send()
+
+
+def plane_of(mesh):
+    devices = mesh.devices.reshape(-1)
+    if mesh.shape["seq"] != devices.size or not hasattr(devices[0], "coords"):
+        return 0
+    places = [(*reversed(d.coords), d.core_on_chip) for d in devices]
+    shape = tuple(max(p[axis] for p in places) + 1 for axis in range(4))
+    plane = shape[1] * shape[2] * shape[3]
+    ordered = [(i // plane, i // 4 % 2, i // 2 % 2, i % 2) for i in range(devices.size)]
+    return plane if shape[1:] == (2, 2, 2) and shape[0] > 1 and places == ordered else 0
 
 
 def solution(mesh):
     count = mesh.shape["seq"]
+    plane = plane_of(mesh)
 
     def shards(tokens, norm_gain, in_weight, in_bias, out_weight, out_bias):
         channels, rows = tokens.shape
-        plan = Plan(count, rows, min(CHUNK, rows // 2), min(TILE, rows // 2))
+        plan = Plan(count, rows, min(CHUNK, rows // 2), min(TILE, rows // 2), plane)
         distant = plan.far * TRACK_CH
         wide = plan.halo + rows
         vmem = pl.BlockSpec(memory_space=pltpu.VMEM)
@@ -197,6 +310,12 @@
             in_specs=[pl.BlockSpec(memory_space=pl.ANY)] + [vmem] * 5,
             out_specs=pl.BlockSpec(memory_space=pl.ANY),
             scratch_shapes=[
+                pltpu.VMEM((BLOCKS, channels, LANES), jnp.float32),
+                pltpu.VMEM(in_weight.shape, jnp.bfloat16),
+                pltpu.VMEM((BLOCKS, in_weight.shape[1], LANES), jnp.float32),
+                pltpu.VMEM((BLOCKS, channels, LANES), jnp.float32),
+                pltpu.VMEM((BLOCKS, TRACK_CH, rows), jnp.bfloat16),
+                pltpu.VMEM((BLOCKS, plan.near, plan.halo), jnp.bfloat16),
                 pltpu.VMEM((plan.near, wide), jnp.bfloat16),
                 pltpu.VMEM((plan.near, wide), jnp.bfloat16),
                 pltpu.VMEM((distant, rows), jnp.bfloat16),
@@ -207,13 +326,17 @@
                 pltpu.SemaphoreType.DMA((BLOCKS, plan.far, plan.chunks)),
                 pltpu.SemaphoreType.DMA((BLOCKS, len(plan.pieces))),
                 pltpu.SemaphoreType.DMA((BLOCKS, len(plan.pieces))),
+                pltpu.SemaphoreType.DMA((BLOCKS, plan.chunks)),
+                pltpu.SemaphoreType.DMA((BLOCKS, plan.chunks)),
+                pltpu.SemaphoreType.DMA((BLOCKS, len(plan.pieces))),
+                pltpu.SemaphoreType.DMA((BLOCKS, len(plan.pieces))),
                 pltpu.SemaphoreType.DMA,
                 pltpu.SemaphoreType.DMA((plan.chunks,)),
             ],
             compiler_params=pltpu.CompilerParams(
                 collective_id=0, has_side_effects=True, vmem_limit_bytes=56 * 2**20
             ),
-        )(tokens, norm_gain[:, :, None], in_weight, in_bias[:, :, None], out_weight, out_bias[:, :, None])
+        )(tokens, norm_gain, jnp.swapaxes(in_weight, 1, 2), in_bias, out_weight, out_bias)
 
     return jax.shard_map(
         shards,

time: 119 us -> 90.8 us (0.76)
  the two profiles are of different devices: /device:TPU:7 before, /device:TPU:8 now
where the time goes in v2:
time: 90.8 us; the launch traced here: 90.6 us
  Pallas kernels  85.4 us (94%)
  local copies, waits for them, and re-layouts  5.22 us (6%)
    pallas_call x1, Pallas kernels, shards(): pl.pallas_call(functools.partial(kernel, plan), out_shape=jax.ShapeDtypeS...  85.4 us
    unnamed x1, local copies, waits for them, and re-layouts  5.22 us

profile of v2, /device:TPU:8, one launch (start us, length us, event | category | flops | bytes accessed | tf_op | source)
XLA Modules:
  0.0 90.6 jit_solution(4204179838059129110)
XLA Ops:
  0.0 85.4 %shard_map.64 = bf16[304,8192]{1,0:T(8,128)(2,1)} custom-call(bf16[304,8192]{1,0:T(8,128)(2,1)} %tokens.1, f32[2,304]{1,0:T(2,128)} %gain_in.1, bf16[2,304,608]{2,1,0:T(8,128)(2,1)} %bitcast.1, f32[2,608]{1,0:T(2,128)} %b_in_in.1, bf16[2,304,608]{2,1,0:T(8,128)(2,1)} %w_out.1, f32[2,304]{1,0:T(2,128)} %b_out_in.1), custom_call_target="tpu_custom_call" | custom-call | tf_op jit(solution)/shard_map/pallas_call | solution.py:307
  85.4 5.2 %copy.8 = bf16[304,8192]{1,0:T(8,128)(2,1)} copy(bf16[304,8192]{1,0:T(8,128)(2,1)} %shard_map.64) | data formatting | bytes 9961472

commit v3 on v2

--- a/solution.py
+++ b/solution.py
@@ -11,8 +11,8 @@
 TRACKS = 19
 BLOCKS = 2
 LANES = 128
-CHUNK = 1024
-TILE = 1024
+CHUNK = 2048
+TILE = 2048
 LAG = 2
 MESH = pl.DeviceIdType.MESH
 

time: 90.8 us -> 81.4 us (0.90)
  Pallas kernels: 85.4 us -> 76 us
    pallas_call x1, Pallas kernels: 85.4 us -> 76 us  [shards(): pl.pallas_call(functools.partial(kernel, plan), out_shape=jax.ShapeDtypeS...]
where the time goes in v3:
time: 81.4 us; the launch traced here: 81.2 us
  Pallas kernels  76 us (93%)
  local copies, waits for them, and re-layouts  5.22 us (6%)
    pallas_call x1, Pallas kernels, shards(): pl.pallas_call(functools.partial(kernel, plan), out_shape=jax.ShapeDtypeS...  76 us
    unnamed x1, local copies, waits for them, and re-layouts  5.22 us

profile of v3, /device:TPU:8, one launch (start us, length us, event | category | flops | bytes accessed | tf_op | source)
XLA Modules:
  0.0 81.2 jit_solution(15625685971469756393)
XLA Ops:
  0.0 76.0 %shard_map.64 = bf16[304,8192]{1,0:T(8,128)(2,1)} custom-call(bf16[304,8192]{1,0:T(8,128)(2,1)} %tokens.1, f32[2,304]{1,0:T(2,128)} %gain_in.1, bf16[2,304,608]{2,1,0:T(8,128)(2,1)} %bitcast.1, f32[2,608]{1,0:T(2,128)} %b_in_in.1, bf16[2,304,608]{2,1,0:T(8,128)(2,1)} %w_out.1, f32[2,304]{1,0:T(2,128)} %b_out_in.1), custom_call_target="tpu_custom_call" | custom-call | tf_op jit(solution)/shard_map/pallas_call | solution.py:307
  76.0 5.2 %copy.8 = bf16[304,8192]{1,0:T(8,128)(2,1)} copy(bf16[304,8192]{1,0:T(8,128)(2,1)} %shard_map.64) | data formatting | bytes 9961472

commit v4 on v3

--- a/solution.py
+++ b/solution.py
@@ -13,7 +13,7 @@
 LANES = 128
 CHUNK = 2048
 TILE = 2048
-LAG = 2
+LAG = 3
 MESH = pl.DeviceIdType.MESH
 
 

time: 81.4 us -> 83.1 us (1.021)
  Pallas kernels: 76 us -> 77.7 us
    pallas_call x1, Pallas kernels: 76 us -> 77.7 us  [shards(): pl.pallas_call(functools.partial(kernel, plan), out_shape=jax.ShapeDtypeS...]
where the time goes in v4:
time: 83.1 us; the launch traced here: 82.9 us
  Pallas kernels  77.7 us (94%)
  local copies, waits for them, and re-layouts  5.22 us (6%)
    pallas_call x1, Pallas kernels, shards(): pl.pallas_call(functools.partial(kernel, plan), out_shape=jax.ShapeDtypeS...  77.7 us
    unnamed x1, local copies, waits for them, and re-layouts  5.22 us

profile of v4, /device:TPU:8, one launch (start us, length us, event | category | flops | bytes accessed | tf_op | source)
XLA Modules:
  0.0 82.9 jit_solution(16065960481949683604)
XLA Ops:
  0.0 77.7 %shard_map.64 = bf16[304,8192]{1,0:T(8,128)(2,1)} custom-call(bf16[304,8192]{1,0:T(8,128)(2,1)} %tokens.1, f32[2,304]{1,0:T(2,128)} %gain_in.1, bf16[2,304,608]{2,1,0:T(8,128)(2,1)} %bitcast.1, f32[2,608]{1,0:T(2,128)} %b_in_in.1, bf16[2,304,608]{2,1,0:T(8,128)(2,1)} %w_out.1, f32[2,304]{1,0:T(2,128)} %b_out_in.1), custom_call_target="tpu_custom_call" | custom-call | tf_op jit(solution)/shard_map/pallas_call | solution.py:307
  77.7 5.2 %copy.8 = bf16[304,8192]{1,0:T(8,128)(2,1)} copy(bf16[304,8192]{1,0:T(8,128)(2,1)} %shard_map.64) | data formatting | bytes 9961472
